TPU v7x, 128 devices: a whole 4x4x4 slice. The times are simulated.
128 devices in a mesh: dp: 8 (over x_hi, z), fsdp: 8 (over y, core), enc: 2 (over x_lo).
Axes of the slice: x: 4 (x_hi: 2, x_lo: 2; x = x_hi * 2 + x_lo), y: 4, z: 4, core: 2. Of those that a mesh axis runs over, the one named last changes fastest.
Arguments:
- queries: bfloat16 [12288, 4096], P(('dp', 'fsdp'), 'enc'), may hold values from -9 to 9
- nbr_keys: bfloat16 [384, 128, 4096], P('dp', 'fsdp', 'enc'), may hold values from -6 to 6
- nbr_values: bfloat16 [384, 128, 4096], P('dp', 'fsdp', 'enc'), may hold values from -6 to 6
- out_proj: bfloat16 [4096, 8192], P('enc', 'fsdp'), may hold values from -0.09375 to 0.09375
- nbr_source: int32 [192, 2], replicated, may hold values from 0 to 7, as said below
- nbr_index: int32 [192, 2], replicated, may hold values from 0 to 47
- nbr_count: int32 [192], replicated, may hold values from 1 to 2
- cotangent: bfloat16 [12288, 8192], P('dp', 'fsdp'), may hold values from -2.390625 to 2.390625
Outputs:
- attended: bfloat16 [12288, 4096], P(('dp', 'fsdp'), 'enc')
- grad_queries: bfloat16 [12288, 4096], P(('dp', 'fsdp'), 'enc')
- grad_keys: bfloat16 [384, 128, 4096], P('dp', 'fsdp', 'enc')
- grad_values: bfloat16 [384, 128, 4096], P('dp', 'fsdp', 'enc')
- grad_proj: bfloat16 [4096, 8192], P('enc', 'fsdp')
Inputs may be any that keep to these rules, and one draw needn't show every extreme that they name: `nbr_source`: among the 6 slots of the spans of one device, no source group is named more than 1 times, and some group exactly 1 times.
All inputs are finite; a program needn't handle non-finite values.
Results may differ from a plain program's by a relative error of at most 0.013.
Values may be sent and summed in bfloat16 or wider, within the bound.
A program may use at most 128 MiB of HBM per device.

v0:
```python
import math
import jax
import jax.numpy as jnp
from jax import lax
from jax.sharding import PartitionSpec as P

HEAD_DIM = 128
SPAN = 64
SLOTS = 2


def local(queries, nbr_keys, nbr_values, out_proj, nbr_source, nbr_index, nbr_count, cotangent):
    dp_count = lax.axis_size("dp")
    fsdp_count = lax.axis_size("fsdp")
    peer_count = dp_count * fsdp_count
    token_rows, width_halved = queries.shape
    heads_here = width_halved // HEAD_DIM
    spans_here = token_rows // SPAN
    slot_count = SLOTS * spans_here
    capacity = (slot_count + dp_count - 1) // dp_count
    group_size, piece_rows, piece_width = nbr_keys.shape
    neighbour_len = piece_rows * fsdp_count
    scale = 1.0 / math.sqrt(HEAD_DIM)
    my_group = lax.axis_index("dp")
    my_place = my_group * fsdp_count + lax.axis_index("fsdp")
    all_sources = nbr_source.reshape(peer_count, slot_count)
    all_indices = nbr_index.reshape(peer_count, slot_count)
    slot_iota = jnp.arange(slot_count, dtype=jnp.int32)
    earlier = slot_iota[None, :] < slot_iota[:, None]
    same_source = all_sources[:, :, None] == all_sources[:, None, :]
    ranks = jnp.sum(jnp.logical_and(same_source, earlier[None]), axis=2)
    cap_iota = jnp.arange(capacity, dtype=jnp.int32)
    selected = jnp.logical_and(
        (all_sources == my_group)[:, :, None], ranks[:, :, None] == cap_iota[None, None, :]
    )
    picked = jnp.sum(jnp.where(selected, all_indices[:, :, None], 0), axis=1)
    present = jnp.any(selected, axis=1)
    flat_pick = picked.reshape(-1)
    send_keys = jnp.take(nbr_keys, flat_pick, axis=0)
    send_values = jnp.take(nbr_values, flat_pick, axis=0)
    got_keys, got_values = (
        lax.all_to_all(send_keys, ("dp", "fsdp"), split_axis=0, concat_axis=0, tiled=True),
        lax.all_to_all(send_values, ("dp", "fsdp"), split_axis=0, concat_axis=0, tiled=True),
    )
    got_keys = got_keys.reshape(dp_count, fsdp_count, capacity, piece_rows, piece_width)
    got_values = got_values.reshape(dp_count, fsdp_count, capacity, piece_rows, piece_width)
    my_sources = lax.dynamic_index_in_dim(all_sources, my_place, 0, keepdims=False)
    my_ranks = lax.dynamic_index_in_dim(ranks, my_place, 0, keepdims=False)
    slot_keys = got_keys[my_sources, :, my_ranks].reshape(
        spans_here, SLOTS * neighbour_len, heads_here, HEAD_DIM
    )
    slot_values = got_values[my_sources, :, my_ranks].reshape(
        spans_here, SLOTS * neighbour_len, heads_here, HEAD_DIM
    )
    local_counts = lax.dynamic_slice_in_dim(nbr_count, my_place * spans_here, spans_here)
    live_keys = jnp.repeat(
        jnp.arange(SLOTS)[None, :] < local_counts[:, None], neighbour_len, axis=1
    )
    query_blocks = queries.reshape(spans_here, SPAN, heads_here, HEAD_DIM)
    scores = (
        jnp.einsum("cqhd,ckhd->chqk", query_blocks, slot_keys, preferred_element_type=jnp.float32)
        * scale
    )
    scores = jnp.where(live_keys[:, None, None, :], scores, -1e30)
    peak = jnp.max(scores, axis=-1, keepdims=True)
    expo = jnp.exp(scores - peak)
    probs = expo / jnp.sum(expo, axis=-1, keepdims=True)
    probs_b = probs.astype(jnp.bfloat16)
    attended = jnp.einsum(
        "chqk,ckhd->cqhd", probs_b, slot_values, preferred_element_type=jnp.float32
    )
    attended = attended.astype(jnp.bfloat16).reshape(token_rows, width_halved)
    gathered = lax.all_gather(attended, "fsdp", axis=0, tiled=True)
    upstream = lax.psum_scatter(
        lax.dot_general(
            cotangent, out_proj, (((1,), (1,)), ((), ())), preferred_element_type=jnp.float32
        ),
        "fsdp",
        scatter_dimension=0,
        tiled=True,
    ).astype(jnp.bfloat16)
    proj_term = lax.dot_general(
        gathered, cotangent, (((0,), (0,)), ((), ())), preferred_element_type=jnp.float32
    )
    grad_proj = lax.psum(proj_term.astype(jnp.bfloat16), "dp")
    upstream_blocks = upstream.reshape(spans_here, SPAN, heads_here, HEAD_DIM)
    probability_gradient = jnp.einsum(
        "cqhd,ckhd->chqk", upstream_blocks, slot_values, preferred_element_type=jnp.float32
    )
    centre = jnp.sum(probs * probability_gradient, axis=-1, keepdims=True)
    dscores = (probs * (probability_gradient - centre) * scale).astype(jnp.bfloat16)
    grad_queries = jnp.einsum(
        "chqk,ckhd->cqhd", dscores, slot_keys, preferred_element_type=jnp.float32
    )
    grad_queries = grad_queries.astype(jnp.bfloat16).reshape(token_rows, width_halved)
    slot_key_grads = jnp.einsum(
        "chqk,cqhd->ckhd", dscores, query_blocks, preferred_element_type=jnp.float32
    ).astype(jnp.bfloat16)
    value_slot_gradients = jnp.einsum(
        "chqk,cqhd->ckhd", probs_b, upstream_blocks, preferred_element_type=jnp.float32
    ).astype(jnp.bfloat16)
    location_table = jnp.logical_and(
        my_sources[None, None, :] == jnp.arange(dp_count, dtype=jnp.int32)[:, None, None],
        my_ranks[None, None, :] == cap_iota[None, :, None],
    ).astype(jnp.bfloat16)
    key_slot_table = slot_key_grads.reshape(slot_count, fsdp_count, piece_rows * piece_width)
    value_slot_table = value_slot_gradients.reshape(
        slot_count, fsdp_count, piece_rows * piece_width
    )
    back_keys = jnp.einsum(
        "vnt,tqg->vqng", location_table, key_slot_table, preferred_element_type=jnp.float32
    ).astype(jnp.bfloat16)
    back_values = jnp.einsum(
        "vnt,tqg->vqng", location_table, value_slot_table, preferred_element_type=jnp.float32
    ).astype(jnp.bfloat16)
    ret_keys, ret_values = (
        lax.all_to_all(
            back_keys.reshape(peer_count * capacity, piece_rows, piece_width),
            ("dp", "fsdp"),
            split_axis=0,
            concat_axis=0,
            tiled=True,
        ),
        lax.all_to_all(
            back_values.reshape(peer_count * capacity, piece_rows, piece_width),
            ("dp", "fsdp"),
            split_axis=0,
            concat_axis=0,
            tiled=True,
        ),
    )
    owner_table = jnp.logical_and(
        flat_pick[None, :] == jnp.arange(group_size, dtype=jnp.int32)[:, None],
        present.reshape(-1)[None, :],
    ).astype(jnp.bfloat16)
    grad_keys = jnp.dot(
        owner_table,
        ret_keys.reshape(peer_count * capacity, piece_rows * piece_width),
        preferred_element_type=jnp.float32,
    )
    grad_values = jnp.dot(
        owner_table,
        ret_values.reshape(peer_count * capacity, piece_rows * piece_width),
        preferred_element_type=jnp.float32,
    )
    grad_keys = grad_keys.astype(jnp.bfloat16).reshape(group_size, piece_rows, piece_width)
    grad_values = grad_values.astype(jnp.bfloat16).reshape(group_size, piece_rows, piece_width)
    return (attended, grad_queries, grad_keys, grad_values, grad_proj)


def solution(mesh):
    placed = (
        P(("dp", "fsdp"), "enc"),
        P("dp", "fsdp", "enc"),
        P("dp", "fsdp", "enc"),
        P("enc", "fsdp"),
        P(),
        P(),
        P(),
        P("dp", "fsdp"),
    )
    return jax.shard_map(
        local,
        mesh=mesh,
        in_specs=placed,
        out_specs=(
            P(("dp", "fsdp"), "enc"),
            P(("dp", "fsdp"), "enc"),
            P("dp", "fsdp", "enc"),
            P("dp", "fsdp", "enc"),
            P("enc", "fsdp"),
        ),
        check_vma=False,
    )
```

profile of v0, /device:TPU:1, one launch (start us, length us, event | category | flops | bytes accessed | tf_op | source)
XLA Modules:
  0.0 503.1 jit_solution(7877312089183280143)
XLA Ops:
  9.1 11.3 %fusion.82 = f32[1536,2048]{1,0:T(8,128)} fusion(bf16[1536,1024]{1,0:T(8,128)(2,1)S(1)} %copy-done, bf16[2048,1024]{1,0:T(8,128)(2,1)} %param.13), kind=kOutput, calls=%fused_computation.97 | convolution fusion | flops 6442450944 | bytes 19922944 | tf_op jit(solution)/shard_map/dot_general | solution.py:75
  22.1 4.7 gather_fusion.3
  26.8 4.7 gather_fusion.2
  31.5 6.4 %broadcast_select_fusion = (bf16[64,16,2048]{2,1,0:T(8,128)(2,1)}, bf16[64,16,2048]{2,1,0:T(8,128)(2,1)S(1)}) fusion(bf16[64,16,2048]{2,1,0:T(8,128)(2,1)} %gather_fusion.3, pred[64]{0:T(512)(128)(4,1)S(1)} %compare_and_fusion.1, bf16[64,16,2048]{2,1,0:T(8,128)(2,1)} %gather_fusion.2), kind=kLoop, calls=%fused_computation.14 | loop fusion | flops 4194304 | bytes 16777280 | tf_op jit(solution)/shard_map/jit(_take)/select_n | solution.py:39
  37.9 73.3 %all_to_all.20 = bf16[64,16,2048]{2,1,0:T(8,128)(2,1)} all-to-all(bf16[64,16,2048]{2,1,0:T(8,128)(2,1)S(1)} %get-tuple-element.9), channel_id=1, replica_groups=mesh['dp'=8,'fsdp'=8,'enc'=2] {'dp','fsdp'}, dimensions={0} | all-to-all | bytes 8388608 | tf_op jit(solution)/shard_map/all_to_all | solution.py:43
  111.3 10.0 %all-to-all-start.1 = ((bf16[64,16,2048]{2,1,0:T(8,128)(2,1)}), bf16[64,16,2048]{2,1,0:T(8,128)(2,1)}, u32[]{:S(2)}, u32[]{:S(2)}) async-start(bf16[64,16,2048]{2,1,0:T(8,128)(2,1)} %get-tuple-element.8), calls=%async_computation.1 | async-start | bytes 8388608 | tf_op jit(solution)/shard_map/all_to_all | solution.py:42
  123.9 4.7 gather_fusion
  133.2 56.3 %all-to-all-done.1 = bf16[64,16,2048]{2,1,0:T(8,128)(2,1)} async-done(((bf16[64,16,2048]{2,1,0:T(8,128)(2,1)}), bf16[64,16,2048]{2,1,0:T(8,128)(2,1)}, u32[]{:S(2)}, u32[]{:S(2)}) %all-to-all-start.1) | async-done | bytes 4194336 | tf_op jit(solution)/shard_map/all_to_all | solution.py:42
  189.4 4.7 gather_fusion.1
  210.5 25.1 %convert_bitcast_fusion.1 = bf16[3,256,16,128]{3,1,2,0:T(8,128)(2,1)} fusion(f32[3,16,64,256]{3,2,1,0:T(8,128)} %fusion.9, bf16[3,64,16,128]{3,2,1,0:T(8,128)(2,1)} %bitcast.119, f32[3,16,64,256]{3,2,1,0:T(8,128)} %copy-done.9, f32[3,16,64]{2,1,0:T(8,128)S(1)} %get-tuple-element.10), kind=kOutput, calls=%fused_computation.22 | convolution fusion | flops 208407808 | bytes 10235904 | tf_op jit(solution)/shard_map/chqk,cqhd->ckhd/dot_general | solution.py:96
  235.7 5.7 %copy.97 = bf16[3,256,16,128]{3,2,1,0:T(8,128)(2,1)} copy(bf16[3,256,16,128]{3,1,2,0:T(8,128)(2,1)} %convert_bitcast_fusion.1) | data formatting | bytes 6291456 | tf_op jit(solution)/shard_map/convert_element_type | solution.py:98
  241.4 6.2 %reshape.273 = bf16[6,8,32768]{2,1,0:T(8,128)(2,1)} reshape(bf16[3,256,16,128]{3,2,1,0:T(8,128)(2,1)} %copy.97) | data formatting | bytes 6291456 | tf_op jit(solution)/shard_map/reshape | solution.py:106
  258.1 9.0 %all-to-all-start.2 = ((bf16[64,16,2048]{2,1,0:T(8,128)(2,1)}), bf16[64,16,2048]{2,1,0:T(8,128)(2,1)}, u32[]{:S(2)}, u32[]{:S(2)}) async-start(bf16[64,16,2048]{2,1,0:T(8,128)(2,1)} %bitcast.105), calls=%async_computation.3 | async-start | bytes 8388608 | tf_op jit(solution)/shard_map/all_to_all | solution.py:117
  267.2 5.0 convert_bitcast_fusion
  272.2 4.9 copy.101
  277.1 5.8 %reshape.277 = bf16[6,8,32768]{2,1,0:T(8,128)(2,1)} reshape(bf16[3,256,16,128]{3,2,1,0:T(8,128)(2,1)} %copy.101) | data formatting | bytes 6291456 | tf_op jit(solution)/shard_map/reshape | solution.py:107
  293.5 24.8 %all-to-all-done.2 = bf16[64,16,2048]{2,1,0:T(8,128)(2,1)} async-done(((bf16[64,16,2048]{2,1,0:T(8,128)(2,1)}), bf16[64,16,2048]{2,1,0:T(8,128)(2,1)}, u32[]{:S(2)}, u32[]{:S(2)}) %all-to-all-start.2) | async-done | bytes 4194336 | tf_op jit(solution)/shard_map/all_to_all | solution.py:117
  318.2 13.6 %all-to-all-start.3 = ((bf16[64,16,2048]{2,1,0:T(8,128)(2,1)}), bf16[64,16,2048]{2,1,0:T(8,128)(2,1)}, u32[]{:S(2)}, u32[]{:S(2)}) async-start(bf16[64,16,2048]{2,1,0:T(8,128)(2,1)} %bitcast.104), calls=%async_computation.4 | async-start | bytes 8388608 | tf_op jit(solution)/shard_map/all_to_all | solution.py:124
  332.0 11.3 %convolution_convert_fusion.4 = bf16[2048,1024]{1,0:T(8,128)(2,1)} fusion(bf16[1536,2048]{1,0:T(8,128)(2,1)} %all-gather.2.cloned.1.call-done, bf16[1536,1024]{1,0:T(8,128)(2,1)S(1)} %copy-done), kind=kOutput, calls=%fused_computation.16 | convolution fusion | flops 6444548096 | bytes 13631488 | tf_op jit(solution)/shard_map/dot_general | solution.py:82
  343.6 23.6 %fusion.41 = bf16[3,64,16,128]{3,1,2,0:T(8,128)(2,1)} fusion(bf16[3,256,16,128]{3,2,1,0:T(8,128)(2,1)} %bitcast.112, f32[3,16,64,256]{3,2,1,0:T(8,128)} %fusion.9, f32[3,16,64,256]{3,2,1,0:T(8,128)} %copy-done.9, f32[3,16,64]{2,1,0:T(8,128)S(1)} %get-tuple-element.10), kind=kOutput, calls=%fused_computation.44 | convolution fusion | flops 207228160 | bytes 10235904 | tf_op jit(solution)/shard_map/chqk,ckhd->cqhd/dot_general | solution.py:92
  379.1 13.4 %all-to-all-done.3 = bf16[64,16,2048]{2,1,0:T(8,128)(2,1)} async-done(((bf16[64,16,2048]{2,1,0:T(8,128)(2,1)}), bf16[64,16,2048]{2,1,0:T(8,128)(2,1)}, u32[]{:S(2)}, u32[]{:S(2)}) %all-to-all-start.3) | async-done | bytes 4194336 | tf_op jit(solution)/shard_map/all_to_all | solution.py:124
  392.4 4.9 copy.114
  401.9 89.6 %all-reduce.2.cloned.1.call-done = bf16[2048,1024]{1,0:T(8,128)(2,1)} async-done(((bf16[2048,1024]{1,0:T(8,128)(2,1)}), bf16[2048,1024]{1,0:T(8,128)(2,1)}) %all-reduce.2.cloned.1.call-update) | async-done | bytes 4194320 | tf_op jit(solution)/shard_map/psum | solution.py:85
  491.5 4.6 copy.149
  (77 shorter events, 64.9 us)
Async XLA Ops:
  7.2 1.9 copy-start
  7.2 197.7 %reduce-scatter.2.cloned.1.call-start = ((), (), s32[]{:S(2)}) async-start(), calls=%async_computation.5 | async-start | bytes 14155776 | tf_op jit(solution)/shard_map/reduce_scatter | solution.py:74
  20.4 0.7 copy-start.6
  20.4 1.4 copy-start.7
  111.3 12.5 %copy-start.8 = (s32[192]{0:T(256)S(1)}, s32[192]{0:T(256)}, u32[]{:S(2)}) copy-start(s32[192]{0:T(256)} %param.16) | copy-start | bytes 2308
  111.3 78.2 %all-to-all-start.1 = ((bf16[64,16,2048]{2,1,0:T(8,128)(2,1)}), bf16[64,16,2048]{2,1,0:T(8,128)(2,1)}, u32[]{:S(2)}, u32[]{:S(2)}) async-start(bf16[64,16,2048]{2,1,0:T(8,128)(2,1)} %get-tuple-element.8), calls=%async_computation.1 | async-start | bytes 8388608 | tf_op jit(solution)/shard_map/all_to_all | solution.py:42
  121.3 210.6 %all-gather.2.cloned.1.call-start = ((), (), s32[]{:S(2)}) async-start(), calls=%async_computation.6 | async-start | bytes 7077888 | tf_op jit(solution)/shard_map/all_gather | solution.py:73
  194.1 3.0 copy-start.4
  197.1 1.7 copy-start.1
  198.8 1.9 copy-start.2
  200.3 2.7 copy-start.9
  204.9 2.8 copy-start.3
  206.8 0.9 copy-start.5
  258.1 60.1 %all-to-all-start.2 = ((bf16[64,16,2048]{2,1,0:T(8,128)(2,1)}), bf16[64,16,2048]{2,1,0:T(8,128)(2,1)}, u32[]{:S(2)}, u32[]{:S(2)}) async-start(bf16[64,16,2048]{2,1,0:T(8,128)(2,1)} %bitcast.105), calls=%async_computation.3 | async-start | bytes 8388608 | tf_op jit(solution)/shard_map/all_to_all | solution.py:117
  318.2 74.2 %all-to-all-start.3 = ((bf16[64,16,2048]{2,1,0:T(8,128)(2,1)}), bf16[64,16,2048]{2,1,0:T(8,128)(2,1)}, u32[]{:S(2)}, u32[]{:S(2)}) async-start(bf16[64,16,2048]{2,1,0:T(8,128)(2,1)} %bitcast.104), calls=%async_computation.4 | async-start | bytes 8388608 | tf_op jit(solution)/shard_map/all_to_all | solution.py:124
  331.9 159.6 %all-reduce.2.cloned.1.call-start = ((), (), s32[]{:S(2)}) async-start(), calls=%async_computation.7 | async-start | bytes 8388608 | tf_op jit(solution)/shard_map/psum | solution.py:85
Sparse Core Ops, SparseCore 0:
  20.5 164.9 reduce-scatter.1
  204.8 41.3 all-gather.1
  343.4 148.0 all-reduce.1
where the time goes:
time: 511 us; the launch traced here: 503 us
  waiting for transfers between devices  184 us (36%)
  local copies, waits for them, and re-layouts  95.6 us (19%)
  matrix products  92.5 us (18%)
  blocking collectives  73.3 us (14%)
  starting transfers between devices  32.8 us (6%)
  between operations  14.5 us (3%)
  other arithmetic  10.3 us (2%)
    psum x1, waiting for transfers between devices, local(): grad_proj = lax.psum(proj_term.astype(jnp.bfloat16), 'dp')  89.6 us
    all_to_all x1, blocking collectives, local(): lax.all_to_all(send_values, ('dp', 'fsdp'), split_axis=0, concat_axis=0,...  73.3 us
    all_to_all x1, waiting for transfers between devices, local(): lax.all_to_all(send_keys, ('dp', 'fsdp'), split_axis=0, concat_axis=0, ti...  56.3 us
    unnamed x34, local copies, waits for them, and re-layouts  46.4 us
    dot_general x1, matrix products, local(): jnp.einsum('chqk,cqhd->ckhd', dscores, query_blocks, preferred_element_ty...  25.1 us
    all_to_all x1, waiting for transfers between devices, local(): lax.all_to_all(back_keys.reshape(peer_count * capacity, piece_rows, piece...  24.8 us
    dot_general x1, matrix products, local(): jnp.einsum('chqk,ckhd->cqhd', dscores, slot_keys, preferred_element_type=...  23.6 us
    all_to_all x1, starting transfers between devices, local(): lax.all_to_all(back_values.reshape(peer_count * capacity, piece_rows, pie...  13.6 us
  transfers between devices with their start and end apart: 6, of which 4 were waited for; matrix products, arithmetic and copies ran while one was open for 35% of the time, Pallas kernels for 0%

commit v1 on v0

--- a/solution.py
+++ b/solution.py
@@ -82,7 +82,7 @@
     proj_term = lax.dot_general(
         gathered, cotangent, (((0,), (0,)), ((), ())), preferred_element_type=jnp.float32
     )
-    grad_proj = lax.psum(proj_term.astype(jnp.bfloat16), "dp")
+    grad_proj = jnp.sum(lax.all_gather(proj_term.astype(jnp.bfloat16), "dp"), axis=0)
     upstream_blocks = upstream.reshape(spans_here, SPAN, heads_here, HEAD_DIM)
     probability_gradient = jnp.einsum(
         "cqhd,ckhd->chqk", upstream_blocks, slot_values, preferred_element_type=jnp.float32

time: 511 us -> 740 us (1.45)
  waiting for transfers between devices: 184 us -> 438 us
  other arithmetic: 10.3 us -> 24.6 us
  local copies, waits for them, and re-layouts: 95.6 us -> 82.4 us
  blocking collectives: 73.3 us -> 63.9 us
  starting transfers between devices: 32.8 us -> 23.8 us
  matrix products: 92.5 us -> 84.4 us
    all_gather x0 -> x1, waiting for transfers between devices: none -> 238 us  [local(): lax.all_gather(proj_term.astype(jnp.bfloat16), 'dp')]
    psum x1 -> x0, waiting for transfers between devices: 89.6 us -> none  [local(): grad_proj = lax.psum(proj_term.astype(jnp.bfloat16), 'dp')]
    reduce_scatter x1, waiting for transfers between devices: 0.02 us -> 62.5 us  [local(): lax.psum_scatter(lax.dot_general(cotangent, out_proj, (((1,), (1,)), ((),...]
    all_gather x1, waiting for transfers between devices: 0.02 us -> 40.7 us  [local(): gathered = lax.all_gather(attended, 'fsdp', axis=0, tiled=True)]
    all_to_all x1, waiting for transfers between devices: 13.4 us -> 34.3 us  [local(): lax.all_to_all(back_values.reshape(peer_count * capacity, piece_rows, pie...]
    all_to_all x1, waiting for transfers between devices: 56.3 us -> 39.3 us  [local(): lax.all_to_all(send_values, ('dp', 'fsdp'), split_axis=0, concat_axis=0,...]
    reduce_sum x0 -> x1, other arithmetic: none -> 14.5 us  [local(): jnp.sum(lax.all_gather(proj_term.astype(jnp.bfloat16), 'dp'), axis=0)]
    all_to_all x1, blocking collectives: 73.3 us -> 63.9 us  [local(): lax.all_to_all(send_keys, ('dp', 'fsdp'), split_axis=0, concat_axis=0, ti...]
  transfers between devices with their start and end apart: 6 -> 6, of which waited for: 4 -> 6; matrix products, arithmetic and copies ran while one was open for 35% -> 20% of each run, Pallas kernels for 0% -> 0%
where the time goes in v1:
time: 740 us; the launch traced here: 731 us
  waiting for transfers between devices  438 us (59%)
  matrix products  84.4 us (11%)
  local copies, waits for them, and re-layouts  82.4 us (11%)
  blocking collectives  63.9 us (9%)
  other arithmetic  24.6 us (3%)
  starting transfers between devices  23.8 us (3%)
  between operations  14.3 us (2%)
    all_gather x1, waiting for transfers between devices, local(): lax.all_gather(proj_term.astype(jnp.bfloat16), 'dp')  238 us
    all_to_all x1, blocking collectives, local(): lax.all_to_all(send_keys, ('dp', 'fsdp'), split_axis=0, concat_axis=0, ti...  63.9 us
    reduce_scatter x1, waiting for transfers between devices, local(): lax.psum_scatter(lax.dot_general(cotangent, out_proj, (((1,), (1,)), ((),...  62.5 us
    all_gather x1, waiting for transfers between devices, local(): gathered = lax.all_gather(attended, 'fsdp', axis=0, tiled=True)  40.7 us
    all_to_all x1, waiting for transfers between devices, local(): lax.all_to_all(send_values, ('dp', 'fsdp'), split_axis=0, concat_axis=0,...  39.3 us
    unnamed x33, local copies, waits for them, and re-layouts  38.2 us
    all_to_all x1, waiting for transfers between devices, local(): lax.all_to_all(back_values.reshape(peer_count * capacity, piece_rows, pie...  34.3 us
    all_to_all x1, waiting for transfers between devices, local(): lax.all_to_all(back_keys.reshape(peer_count * capacity, piece_rows, piece...  23.3 us
  transfers between devices with their start and end apart: 6, of which 6 were waited for; matrix products, arithmetic and copies ran while one was open for 20% of the time, Pallas kernels for 0%

profile of v1, /device:TPU:1, one launch (start us, length us, event | category | flops | bytes accessed | tf_op | source)
XLA Modules:
  0.0 731.3 jit_solution(3055345593283386107)
XLA Ops:
  10.5 4.6 gather_fusion.2
  15.1 4.7 gather_fusion.3
  19.8 5.2 broadcast_select_fusion
  25.1 63.9 %all_to_all.20 = bf16[64,16,2048]{2,1,0:T(8,128)(2,1)} all-to-all(bf16[64,16,2048]{2,1,0:T(8,128)(2,1)S(1)} %get-tuple-element.8), channel_id=1, replica_groups=mesh['dp'=8,'fsdp'=8,'enc'=2] {'dp','fsdp'}, dimensions={0} | all-to-all | bytes 8388608 | tf_op jit(solution)/shard_map/all_to_all | solution.py:42
  88.9 7.3 all-to-all-start
  98.8 4.7 gather_fusion.1
  108.1 39.3 %all-to-all-done = bf16[64,16,2048]{2,1,0:T(8,128)(2,1)} async-done(((bf16[64,16,2048]{2,1,0:T(8,128)(2,1)}), bf16[64,16,2048]{2,1,0:T(8,128)(2,1)}, u32[]{:S(2)}, u32[]{:S(2)}) %all-to-all-start) | async-done | bytes 4194336 | tf_op jit(solution)/shard_map/all_to_all | solution.py:43
  147.4 4.7 gather_fusion
  161.8 11.3 %fusion.82 = f32[1536,2048]{1,0:T(8,128)} fusion(bf16[1536,1024]{1,0:T(8,128)(2,1)S(1)} %copy-done, bf16[2048,1024]{1,0:T(8,128)(2,1)} %param.13), kind=kOutput, calls=%fused_computation.97 | convolution fusion | flops 6442450944 | bytes 19922944 | tf_op jit(solution)/shard_map/dot_general | solution.py:75
  173.3 40.7 %all-gather.4.cloned.1.call-done = bf16[1536,2048]{1,0:T(8,128)(2,1)} async-done(((bf16[192,2048]{1,0:T(8,128)(2,1)}), bf16[1536,2048]{1,0:T(8,128)(2,1)}) %all-gather.4.cloned.1.call-update) | async-done | bytes 6291472 | tf_op jit(solution)/shard_map/all_gather | solution.py:73
  214.0 11.2 %convolution_convert_fusion.4 = bf16[2048,1024]{1,0:T(8,128)(2,1)} fusion(bf16[1536,2048]{1,0:T(8,128)(2,1)} %all-gather.4.cloned.1.call-done, bf16[1536,1024]{1,0:T(8,128)(2,1)S(1)} %copy-done), kind=kOutput, calls=%fused_computation.16 | convolution fusion | flops 6444548096 | bytes 13631488 | tf_op jit(solution)/shard_map/dot_general | solution.py:82
  225.4 62.5 %reduce-scatter.2.cloned.1.call-done = f32[192,2048]{1,0:T(8,128)} async-done(((f32[1536,2048]{1,0:T(8,128)}), f32[192,2048]{1,0:T(8,128)}) %reduce-scatter.2.cloned.1.call-update) | async-done | bytes 1572880 | tf_op jit(solution)/shard_map/reduce_scatter | solution.py:74
  289.7 5.0 convert_bitcast_fusion
  294.7 4.9 copy.101
  312.7 10.1 %all-to-all-start.3 = ((bf16[64,16,2048]{2,1,0:T(8,128)(2,1)}), bf16[64,16,2048]{2,1,0:T(8,128)(2,1)}, u32[]{:S(2)}, u32[]{:S(2)}) async-start(bf16[64,16,2048]{2,1,0:T(8,128)(2,1)} %bitcast.107), calls=%async_computation.4 | async-start | bytes 8388608 | tf_op jit(solution)/shard_map/all_to_all | solution.py:124
  326.9 23.1 %convert_bitcast_fusion.1 = bf16[3,256,16,128]{3,1,2,0:T(8,128)(2,1)S(1)} fusion(f32[3,16,64,256]{3,2,1,0:T(8,128)} %fusion.9, bf16[3,64,16,128]{3,2,1,0:T(8,128)(2,1)} %bitcast.121, f32[3,16,64,256]{3,2,1,0:T(8,128)} %copy-done.9, f32[3,16,64]{2,1,0:T(8,128)S(1)} %get-tuple-element.10), kind=kOutput, calls=%fused_computation.22 | convolution fusion | flops 208407808 | bytes 10235904 | tf_op jit(solution)/shard_map/chqk,cqhd->ckhd/dot_general | solution.py:96
  366.9 34.3 %all-to-all-done.3 = bf16[64,16,2048]{2,1,0:T(8,128)(2,1)} async-done(((bf16[64,16,2048]{2,1,0:T(8,128)(2,1)}), bf16[64,16,2048]{2,1,0:T(8,128)(2,1)}, u32[]{:S(2)}, u32[]{:S(2)}) %all-to-all-start.3) | async-done | bytes 4194336 | tf_op jit(solution)/shard_map/all_to_all | solution.py:124
  401.2 6.1 all-to-all-start.2
  407.6 20.4 %fusion.41 = bf16[3,64,16,128]{3,1,2,0:T(8,128)(2,1)} fusion(bf16[3,256,16,128]{3,2,1,0:T(8,128)(2,1)S(1)} %bitcast.114, f32[3,16,64,256]{3,2,1,0:T(8,128)} %fusion.9, f32[3,16,64,256]{3,2,1,0:T(8,128)} %copy-done.9, f32[3,16,64]{2,1,0:T(8,128)S(1)} %get-tuple-element.10), kind=kOutput, calls=%fused_computation.44 | convolution fusion | flops 207228160 | bytes 10235904 | tf_op jit(solution)/shard_map/chqk,ckhd->cqhd/dot_general | solution.py:92
  430.7 4.6 copy.114
  439.9 23.3 %all-to-all-done.2 = bf16[64,16,2048]{2,1,0:T(8,128)(2,1)} async-done(((bf16[64,16,2048]{2,1,0:T(8,128)(2,1)}), bf16[64,16,2048]{2,1,0:T(8,128)(2,1)}, u32[]{:S(2)}, u32[]{:S(2)}) %all-to-all-start.2) | async-done | bytes 4194336 | tf_op jit(solution)/shard_map/all_to_all | solution.py:117
  463.1 4.6 copy.111
  472.3 237.9 %all-gather.6.cloned.1.call-done = bf16[16384,1024]{1,0:T(8,128)(2,1)} async-done(((bf16[2048,1024]{1,0:T(8,128)(2,1)}), bf16[16384,1024]{1,0:T(8,128)(2,1)}) %all-gather.6.cloned.1.call-update) | async-done | bytes 33554448 | tf_op jit(solution)/shard_map/all_gather | solution.py:85
  710.2 14.5 %reduce_sum.61 = bf16[2048,1024]{1,0:T(8,128)(2,1)} reduce(bf16[8,2048,1024]{2,1,0:T(8,128)(2,1)} %bitcast.105, bf16[]{:T(256)} %constant.52.clone.1), dimensions={0}, to_apply=%region_9.11 | reduce | flops 14680064 | bytes 37748736 | tf_op jit(solution)/shard_map/reduce_sum | solution.py:85
  (77 shorter events, 68.3 us)
Async XLA Ops:
  7.2 154.6 %copy-start = (bf16[1536,1024]{1,0:T(8,128)(2,1)S(1)}, bf16[1536,1024]{1,0:T(8,128)(2,1)}, u32[]{:S(2)}) copy-start(bf16[1536,1024]{1,0:T(8,128)(2,1)} %param.17) | copy-start | bytes 9437188
  88.9 9.7 %copy-start.8 = (s32[192]{0:T(256)S(1)}, s32[192]{0:T(256)}, u32[]{:S(2)}) copy-start(s32[192]{0:T(256)} %param.16) | copy-start | bytes 2308
  88.9 58.4 %all-to-all-start = ((bf16[64,16,2048]{2,1,0:T(8,128)(2,1)}), bf16[64,16,2048]{2,1,0:T(8,128)(2,1)}, u32[]{:S(2)}, u32[]{:S(2)}) async-start(bf16[64,16,2048]{2,1,0:T(8,128)(2,1)} %get-tuple-element.9), calls=%async_computation | async-start | bytes 8388608 | tf_op jit(solution)/shard_map/all_to_all | solution.py:43
  96.2 117.8 %all-gather.4.cloned.1.call-start = ((), (), s32[]{:S(2)}) async-start(), calls=%async_computation.6 | async-start | bytes 7077888 | tf_op jit(solution)/shard_map/all_gather | solution.py:73
  152.0 3.1 copy-start.2
  152.0 3.1 copy-start.6
  155.1 2.6 copy-start.4
  157.7 2.4 copy-start.9
  161.7 126.2 %reduce-scatter.2.cloned.1.call-start = ((), (), s32[]{:S(2)}) async-start(), calls=%async_computation.5 | async-start | bytes 14155776 | tf_op jit(solution)/shard_map/reduce_scatter | solution.py:74
  173.1 537.1 %all-gather.6.cloned.1.call-start = ((), (), s32[]{:S(2)}) async-start(), calls=%async_computation.7 | async-start | bytes 37748736 | tf_op jit(solution)/shard_map/all_gather | solution.py:85
  289.7 5.0 copy-start.7
  312.7 10.2 %copy-start.5 = (bf16[96,8,16,128]{3,2,1,0:T(8,128)(2,1)S(1)}, bf16[96,8,16,128]{3,2,1,0:T(8,128)(2,1)}, u32[]{:S(2)}) copy-start(bf16[96,8,16,128]{3,2,1,0:T(8,128)(2,1)} %copy-done.4) | copy-start | bytes 9437188
  312.7 88.5 %all-to-all-start.3 = ((bf16[64,16,2048]{2,1,0:T(8,128)(2,1)}), bf16[64,16,2048]{2,1,0:T(8,128)(2,1)}, u32[]{:S(2)}, u32[]{:S(2)}) async-start(bf16[64,16,2048]{2,1,0:T(8,128)(2,1)} %bitcast.107), calls=%async_computation.4 | async-start | bytes 8388608 | tf_op jit(solution)/shard_map/all_to_all | solution.py:124
  401.2 6.3 copy-start.3
  401.2 61.9 %all-to-all-start.2 = ((bf16[64,16,2048]{2,1,0:T(8,128)(2,1)}), bf16[64,16,2048]{2,1,0:T(8,128)(2,1)}, u32[]{:S(2)}, u32[]{:S(2)}) async-start(bf16[64,16,2048]{2,1,0:T(8,128)(2,1)} %bitcast.106), calls=%async_computation.3 | async-start | bytes 8388608 | tf_op jit(solution)/shard_map/all_to_all | solution.py:117
  710.2 14.5 %copy-start.1 = (bf16[1536,1024]{1,0:T(8,128)(2,1)S(1)}, bf16[1536,1024]{1,0:T(8,128)(2,1)}, u32[]{:S(2)}) copy-start(bf16[1536,1024]{1,0:T(8,128)(2,1)} %param.17) | copy-start | bytes 9437188
Sparse Core Ops, SparseCore 0:
  161.9 52.0 all-gather.3
  216.4 71.4 reduce-scatter.1
  290.3 419.8 all-gather.5
